TPU v7x, 512 devices: a whole 4x8x8 slice. The times are simulated.
512 devices in a mesh: wide: 64 (over y, z_hi, core), batch: 8 (over z_lo, x).
Axes of the slice: x: 4, y: 8, z: 8 (z_hi: 4, z_lo: 2; z = z_hi * 2 + z_lo), core: 2. Of those that a mesh axis runs over, the one named last changes fastest.
Arguments:
- integrals: bfloat16 [1536, 64, 640], P('wide'), may hold values from -0.8984375 to 0.8984375
- vir_coeff: bfloat16 [640, 512], P(None, 'batch'), may hold values from -0.25 to 0.25
- occ_energy: float32 [64], replicated, may hold values from -1.6 to -0.4
- vir_energy: float32 [512], replicated, may hold values from 0.2 to 3
- kappas: float32 [8], replicated, may hold values from 0.1 to 3
Outputs:
- density: bfloat16 [8, 64, 512, 1536], P(None, 'wide', 'batch')
All inputs are finite; a program needn't handle non-finite values.
Results may differ from a plain program's by a relative error of at most 0.0051.
Values may be sent and summed in bfloat16 or wider, within the bound.
A program may use at most 64 MiB of HBM per device.

v0:
```python
import jax
import jax.numpy as jnp
from jax import lax
from jax.sharding import PartitionSpec as P

HALF = 2


def from_behind(shard, axis, by):
    peers = lax.axis_size(axis)
    return lax.ppermute(shard, axis, [(i, (i + by) % peers) for i in range(peers)])


def pair_density(own_slice, partner, own_energy, partner_energy, row_energy, vir_energy, kappas):
    coulomb = lax.dot_general(
        own_slice, partner, (((0,), (0,)), ((), ())), preferred_element_type=jnp.float32
    )
    denominator = row_energy[:, None] + vir_energy[None, :] - own_energy - partner_energy
    damping = 1.0 - jnp.exp(-kappas[:, None, None] * denominator[None])
    amplitude = (-coulomb[None] * (damping * damping) / denominator[None]).astype(jnp.bfloat16)
    flat = amplitude.reshape(-1, amplitude.shape[2])
    density = lax.dot_general(
        flat, partner, (((1,), (1,)), ((), ())), preferred_element_type=jnp.float32
    )
    return density.reshape(kappas.shape[0], own_slice.shape[1], partner.shape[0])


def on_device(integrals, vir_coeff, occ_energy, vir_energy, kappas):
    aux_local, occ_count, basis = integrals.shape
    vir_local = vir_coeff.shape[1]
    batch_index = lax.axis_index("batch")
    wide_index = lax.axis_index("wide")
    flat_ints = integrals.reshape(aux_local * occ_count, basis)
    row_energy = lax.dynamic_slice_in_dim(vir_energy, batch_index * vir_local, vir_local, 0)
    own_energy = lax.dynamic_slice_in_dim(occ_energy, wide_index, 1, 0)[0]

    def term(partner, offset, own_slice):
        partner_index = (wide_index + offset) % occ_count
        partner_energy = lax.dynamic_slice_in_dim(occ_energy, partner_index, 1, 0)[0]
        return pair_density(
            own_slice, partner, own_energy, partner_energy, row_energy, vir_energy, kappas
        )

    transformed = jnp.dot(flat_ints, vir_coeff, preferred_element_type=jnp.float32).astype(
        jnp.bfloat16
    )
    transformed = transformed.reshape(aux_local, occ_count, vir_local)
    own_slice = lax.all_to_all(transformed, "wide", split_axis=1, concat_axis=0, tiled=True)[
        :, 0, :
    ]
    own_full = lax.all_gather(own_slice, "batch", axis=1, tiled=True)
    partner = from_behind(own_full, "wide", HALF)
    density = term(partner, -HALF, own_slice)
    for offset in range(1 - HALF, HALF + 1):
        partner = from_behind(partner, "wide", -1)
        density = density + term(partner, offset, own_slice)
    return density.astype(jnp.bfloat16)[:, None, :, :]


def solution(mesh):
    return jax.shard_map(
        on_device,
        mesh=mesh,
        in_specs=(P("wide", None, None), P(None, "batch"), P(), P(), P()),
        out_specs=P(None, "wide", "batch", None),
        check_vma=False,
    )
```

profile of v0, /device:TPU:31, one launch (start us, length us, event | category | flops | bytes accessed | tf_op | source)
XLA Modules:
  0.0 345.7 jit_solution(11318890819423333155)
XLA Ops:
  6.5 0.0 copy-start
  6.5 0.0 all-gather.2.cloned.1.call-start
  6.5 1.5 copy-done
  8.1 1.6 convolution_convert_fusion
  9.7 0.2 reshape.201
  9.9 0.4 copy.16
  10.3 0.2 reshape.207
  10.6 28.0 %all_to_all.15 = bf16[64,2,768]{2,1,0:T(2,128)(2,1)S(1)} all-to-all(bf16[64,2,768]{2,1,0:T(2,128)(2,1)S(1)} %reshape.207), channel_id=1, replica_groups=mesh['wide'=64,'batch'=8] {'wide'}, dimensions={0} | all-to-all | bytes 393216 | tf_op jit(solution)/shard_map/all_to_all | solution.py:48
  38.6 0.3 reshape.208
  38.9 0.8 copy.17
  39.7 0.0 all-gather.2.cloned.1.call-update
  39.7 0.0 copy-start.7
  39.8 0.0 copy-start.6
  39.8 0.0 copy-start.5
  39.8 34.2 %all-gather.2.cloned.1.call-done = bf16[1536,512]{0,1:T(8,128)(2,1)} async-done(((bf16[1536,64]{0,1:T(8,128)(2,1)}), bf16[1536,512]{0,1:T(8,128)(2,1)}) %all-gather.2.cloned.1.call-update) | async-done | bytes 1572880 | tf_op jit(solution)/shard_map/all_gather | solution.py:51
  73.9 2.6 copy.18
  76.5 4.3 %collective-permute-start = (bf16[1536,512]{1,0:T(8,128)(2,1)}, bf16[1536,512]{1,0:T(8,128)(2,1)S(1)}, u32[]{:S(2)}, u32[]{:S(2)}) collective-permute-start(bf16[1536,512]{1,0:T(8,128)(2,1)} %copy.18), channel_id=1, source_target_pairs={{0,16},{8,24},{16,32},{24,40},{32,48},{40,56},{48,64},{56,72},{64,... | collective-permute-start | bytes 4718600 | tf_op jit(solution)/shard_map/ppermute | solution.py:11
  80.9 56.8 %collective-permute-done = bf16[1536,512]{1,0:T(8,128)(2,1)S(1)} collective-permute-done((bf16[1536,512]{1,0:T(8,128)(2,1)}, bf16[1536,512]{1,0:T(8,128)(2,1)S(1)}, u32[]{:S(2)}, u32[]{:S(2)}) %collective-permute-start) | collective-permute-done | bytes 1572896 | tf_op jit(solution)/shard_map/ppermute | solution.py:11
  137.7 0.0 copy-start.3
  137.7 9.7 %collective-permute-start.1 = (bf16[1536,512]{1,0:T(8,128)(2,1)S(1)}, bf16[1536,512]{1,0:T(8,128)(2,1)S(1)}, u32[]{:S(2)}, u32[]{:S(2)}) collective-permute-start(bf16[1536,512]{1,0:T(8,128)(2,1)S(1)} %collective-permute-done), channel_id=1, source_target_pairs={{0,504},{8,0},{16,8},{24,16},{32,24},{40,32},{48,40},{56,48},{64,5... | collective-permute-start | bytes 4718600 | tf_op jit(solution)/shard_map/ppermute | solution.py:11
  147.4 61.3 %collective-permute-done.1 = bf16[1536,512]{1,0:T(8,128)(2,1)S(1)} collective-permute-done((bf16[1536,512]{1,0:T(8,128)(2,1)S(1)}, bf16[1536,512]{1,0:T(8,128)(2,1)S(1)}, u32[]{:S(2)}, u32[]{:S(2)}) %collective-permute-start.1) | collective-permute-done | bytes 1572896 | tf_op jit(solution)/shard_map/ppermute | solution.py:11
  208.8 0.0 copy-start.1
  208.8 1.2 copy-done.1
  210.0 1.9 collective-permute-start.2
  211.9 51.3 %collective-permute-done.2 = bf16[1536,512]{1,0:T(8,128)(2,1)} collective-permute-done((bf16[1536,512]{1,0:T(8,128)(2,1)S(1)}, bf16[1536,512]{1,0:T(8,128)(2,1)}, u32[]{:S(2)}, u32[]{:S(2)}) %collective-permute-start.2) | collective-permute-done | bytes 1572896 | tf_op jit(solution)/shard_map/ppermute | solution.py:11
  263.2 0.0 copy-done.3
  263.2 1.9 collective-permute-start.3
  265.2 0.0 copy-done.7
  265.2 0.0 copy-done.6
  265.2 0.0 copy-start.4
  265.3 0.1 dynamic_slice.21
  265.3 0.0 copy-done.5
  265.3 0.7 fusion.38
  266.0 3.7 %fusion.28 = (f32[64,512]{1,0:T(8,128)S(1)}, f32[64,512]{1,0:T(8,128)S(1)}, f32[64,512]{1,0:T(8,128)S(1)}, f32[64,512]{1,0:T(8,128)S(1)}, f32[64,512]{1,0:T(8,128)S(1)}) fusion(f32[]{:T(128)} %bitcast.15, f32[]{:T(128)} %bitcast.6, f32[512]{0:T(512)S(1)} %copy-done.6, f32[64]{0:T(128)S(1)} %dynamic_slice.21, f32[]{:T(128)} %bitcast.13, f32[]{:T(128)} %bitcast.11, ...), kind=kLoop, calls=%fused_computation.44 | loop fusion | flops 229376 | bytes 657688 | tf_op jit(solution)/shard_map/sub | solution.py:18
  269.8 1.8 convolution_negate_fusion.4
  271.6 0.0 copy-done.4
  271.6 0.0 copy-start.2
  271.6 1.1 fusion.6
  272.7 0.3 copy-done.2
  273.0 0.4 convolution_negate_fusion.3
  273.4 38.6 %collective-permute-done.3 = bf16[1536,512]{1,0:T(8,128)(2,1)} collective-permute-done((bf16[1536,512]{1,0:T(8,128)(2,1)}, bf16[1536,512]{1,0:T(8,128)(2,1)}, u32[]{:S(2)}, u32[]{:S(2)}) %collective-permute-start.3) | collective-permute-done | bytes 1572896 | tf_op jit(solution)/shard_map/ppermute | solution.py:11
  312.0 1.9 collective-permute-start.4
  313.9 1.1 convolution_add_fusion.3
  315.0 1.8 convolution_negate_fusion.2
  316.8 2.5 convolution_add_fusion.2
  319.3 1.8 convolution_negate_fusion.1
  321.1 2.5 convolution_add_fusion.1
  323.6 12.6 %collective-permute-done.4 = bf16[1536,512]{1,0:T(8,128)(2,1)S(1)} collective-permute-done((bf16[1536,512]{1,0:T(8,128)(2,1)}, bf16[1536,512]{1,0:T(8,128)(2,1)S(1)}, u32[]{:S(2)}, u32[]{:S(2)}) %collective-permute-start.4) | collective-permute-done | bytes 1572896 | tf_op jit(solution)/shard_map/ppermute | solution.py:11
  336.2 0.4 convolution_negate_fusion
  336.6 2.2 fusion.1
  (1 shorter events, 0.0 us)
Async XLA Ops:
  6.5 1.5 copy-start
  6.5 67.4 %all-gather.2.cloned.1.call-start = ((), (), s32[]{:S(2)}) async-start(), calls=%async_computation.1 | async-start | bytes 1769472 | tf_op jit(solution)/shard_map/all_gather | solution.py:51
  39.7 225.4 %copy-start.7 = (f32[8]{0:T(128)S(1)}, f32[8]{0:T(128)}, u32[]{:S(2)}) copy-start(f32[8]{0:T(128)} %param.9) | copy-start | bytes 100
  39.8 225.5 %copy-start.6 = (f32[512]{0:T(512)S(1)}, f32[512]{0:T(512)}, u32[]{:S(2)}) copy-start(f32[512]{0:T(512)} %param.8) | copy-start | bytes 6148
  39.8 225.6 %copy-start.5 = (f32[64]{0:T(128)S(1)}, f32[64]{0:T(128)}, u32[]{:S(2)}) copy-start(f32[64]{0:T(128)} %param.7) | copy-start | bytes 772
  76.5 61.2 %collective-permute-start = (bf16[1536,512]{1,0:T(8,128)(2,1)}, bf16[1536,512]{1,0:T(8,128)(2,1)S(1)}, u32[]{:S(2)}, u32[]{:S(2)}) collective-permute-start(bf16[1536,512]{1,0:T(8,128)(2,1)} %copy.18), channel_id=1, source_target_pairs={{0,16},{8,24},{16,32},{24,40},{32,48},{40,56},{48,64},{56,72},{64,... | collective-permute-start | bytes 4718600 | tf_op jit(solution)/shard_map/ppermute | solution.py:11
  137.7 125.5 %copy-start.3 = (bf16[1536,512]{1,0:T(8,128)(2,1)}, bf16[1536,512]{1,0:T(8,128)(2,1)S(1)}, u32[]{:S(2)}) copy-start(bf16[1536,512]{1,0:T(8,128)(2,1)S(1)} %collective-permute-done) | copy-start | bytes 4718596
  137.7 71.1 %collective-permute-start.1 = (bf16[1536,512]{1,0:T(8,128)(2,1)S(1)}, bf16[1536,512]{1,0:T(8,128)(2,1)S(1)}, u32[]{:S(2)}, u32[]{:S(2)}) collective-permute-start(bf16[1536,512]{1,0:T(8,128)(2,1)S(1)} %collective-permute-done), channel_id=1, source_target_pairs={{0,504},{8,0},{16,8},{24,16},{32,24},{40,32},{48,40},{56,48},{64,5... | collective-permute-start | bytes 4718600 | tf_op jit(solution)/shard_map/ppermute | solution.py:11
  208.8 1.2 copy-start.1
  210.0 53.2 %collective-permute-start.2 = (bf16[1536,512]{1,0:T(8,128)(2,1)S(1)}, bf16[1536,512]{1,0:T(8,128)(2,1)}, u32[]{:S(2)}, u32[]{:S(2)}) collective-permute-start(bf16[1536,512]{1,0:T(8,128)(2,1)S(1)} %collective-permute-done.1), channel_id=1, source_target_pairs={{0,504},{8,0},{16,8},{24,16},{32,24},{40,32},{48,40},{56,48},{64,5... | collective-permute-start | bytes 4718600 | tf_op jit(solution)/shard_map/ppermute | solution.py:11
  263.2 48.8 %collective-permute-start.3 = (bf16[1536,512]{1,0:T(8,128)(2,1)}, bf16[1536,512]{1,0:T(8,128)(2,1)}, u32[]{:S(2)}, u32[]{:S(2)}) collective-permute-start(bf16[1536,512]{1,0:T(8,128)(2,1)} %collective-permute-done.2), channel_id=1, source_target_pairs={{0,504},{8,0},{16,8},{24,16},{32,24},{40,32},{48,40},{56,48},{64,5... | collective-permute-start | bytes 4718600 | tf_op jit(solution)/shard_map/ppermute | solution.py:11
  265.2 6.3 %copy-start.4 = (bf16[1536,512]{1,0:T(8,128)(2,1)S(1)}, bf16[1536,512]{1,0:T(8,128)(2,1)}, u32[]{:S(2)}) copy-start(bf16[1536,512]{1,0:T(8,128)(2,1)} %copy-done.3) | copy-start | bytes 4718596
  271.6 1.4 copy-start.2
  312.0 24.2 %collective-permute-start.4 = (bf16[1536,512]{1,0:T(8,128)(2,1)}, bf16[1536,512]{1,0:T(8,128)(2,1)S(1)}, u32[]{:S(2)}, u32[]{:S(2)}) collective-permute-start(bf16[1536,512]{1,0:T(8,128)(2,1)} %collective-permute-done.3), channel_id=1, source_target_pairs={{0,504},{8,0},{16,8},{24,16},{32,24},{40,32},{48,40},{56,48},{64,5... | collective-permute-start | bytes 4718600 | tf_op jit(solution)/shard_map/ppermute | solution.py:11
Sparse Core Ops, SparseCore 0:
  39.9 34.0 all-gather.1
where the time goes:
time: 346 us
  waiting for transfers between devices  255 us (74%)
  blocking collectives  28 us (8%)
  starting transfers between devices  19.8 us (6%)
  matrix products  17.2 us (5%)
  between operations  13.7 us (4%)
  local copies, waits for them, and re-layouts  8.39 us (2%)
  other arithmetic  3.73 us (1%)
    ppermute x5, waiting for transfers between devices, from_behind(): lax.ppermute(shard, axis, [(i, (i + by) % peers) for i in range(peers)])  221 us
    all_gather x1, waiting for transfers between devices, on_device(): own_full = lax.all_gather(own_slice, 'batch', axis=1, tiled=True)  34.2 us
    all_to_all x1, blocking collectives, on_device(): lax.all_to_all(transformed, 'wide', split_axis=1, concat_axis=0, tiled=True)  28 us
    ppermute x5, starting transfers between devices, from_behind(): lax.ppermute(shard, axis, [(i, (i + by) % peers) for i in range(peers)])  19.8 us
    dot_general x5, matrix products, pair_density(): lax.dot_general(flat, partner, (((1,), (1,)), ((), ())), preferred_elemen...  9.32 us
  transfers between devices with their start and end apart: 6, of which 6 were waited for; matrix products, arithmetic and copies ran while one was open for 5% of the time, Pallas kernels for 0%

commit v1 on v0

v1 whole, which is shorter than its diff:
```python
import functools

import jax
import jax.numpy as jnp
from jax import lax
from jax.experimental import pallas as pl
from jax.experimental.pallas import tpu as pltpu
from jax.sharding import PartitionSpec as P

HALF = 2
NX = 4
MESH = pl.DeviceIdType.MESH
ORDER = (1, 0, 2)


def kernel(
    ny, nz, ints_ref, coef_ref, vir_ref, occ_ref, kap_ref, out_ref,
    full, mine, rows, gath, tit, row_exp, vir2, kvec, row_e, amp, acc,
    local_sem, y_send, y_recv, z_send, z_recv, g_send, g_recv, s_send, s_recv,
):
    wide = lax.axis_index("wide")
    batch = lax.axis_index("batch")
    core = lax.rem(wide, 2)
    zh = lax.rem(wide // 2, nz)
    y = wide // (2 * nz)
    x = lax.rem(batch, NX)
    zl = batch // NX
    pairs = ny * nz
    own_pair = wide // 2
    naux = out_ref.shape[1]

    def at_wide(yy, zz, cc):
        return {"wide": (yy * nz + zz) * 2 + cc, "batch": batch}

    def at_batch(dx, dz):
        return lax.rem(zl + dz, 2) * NX + lax.rem(x + dx + NX, NX)

    def dev_batch(dx, dz):
        return {"wide": wide, "batch": at_batch(dx, dz)}

    sibling = at_wide(y, zh, 1 - core)
    left, right, over = dev_batch(-1, 0), dev_batch(1, 0), dev_batch(0, 1)

    barrier = pltpu.get_barrier_semaphore()
    peers = [at_wide(lax.rem(y + d, ny), zh, core) for d in range(1, ny)]
    peers += [at_wide(y, lax.rem(zh + d, nz), core) for d in range(1, nz)]
    peers += [left, right, over, sibling]
    for peer in peers:
        pl.semaphore_signal(barrier, inc=1, device_id=peer, device_id_type=MESH)

    coef2 = jnp.concatenate([coef_ref[...], coef_ref[...]], axis=1)
    steps = 4
    tall = full.shape[0] // steps

    def transform(s, carry):
        at = pl.multiple_of(s * tall, tall)
        full[pl.ds(at, tall), :] = jnp.dot(
            ints_ref[pl.ds(at, tall), :], coef2, preferred_element_type=jnp.float32
        )
        return carry

    lax.fori_loop(0, steps, transform, 0)
    nocc = 2 * pairs
    nrow = full.shape[0] // nocc
    low = lax.broadcasted_iota(jnp.int32, (nrow, 128), 1) < 64
    for m in range(pairs):
        even = full[pl.ds(2 * m, nrow, stride=nocc), :]
        odd = full[pl.ds(2 * m + 1, nrow, stride=nocc), :]
        tile = jnp.where(low, even, odd).reshape(nrow // 8, 8, 128).astype(jnp.bfloat16)
        mine[m + 1] = tile
        if m == 0:
            mine[pairs + 1] = tile
        if m == pairs - 1:
            mine[0] = tile

    pl.semaphore_wait(barrier, len(peers))

    def y_copy(yy, src_y):
        return pltpu.make_async_remote_copy(
            src_ref=mine.at[pl.ds(nz * yy, nz + 2)],
            dst_ref=rows.at[:, src_y],
            send_sem=y_send.at[yy],
            recv_sem=y_recv.at[src_y],
            device_id=at_wide(yy, zh, core),
            device_id_type=MESH,
        )

    far_first = sorted(range(1, ny), key=lambda d: -min(d, ny - d))
    for d in far_first:
        y_copy(lax.rem(y + d, ny), y).start()
    y_own = pltpu.make_async_copy(mine.at[pl.ds(nz * y, nz + 2)], rows.at[:, y], local_sem.at[0])
    y_own.start()

    for b in range(2 * NX):
        part = vir_ref[:, b * 64 : (b + 1) * 64]
        vir2[pl.ds(b, 1), :] = jnp.concatenate([part, part], axis=1)
    qs = lax.broadcasted_iota(jnp.int32, (8, 128), 0)
    kv = jnp.zeros((8, 128), jnp.float32)
    for q in range(8):
        kv = jnp.where(qs == q, kap_ref[q], kv)
    kvec[...] = kv
    columns = jnp.transpose(vir2[...])
    pick = lax.broadcasted_iota(jnp.int32, (128, 8), 1) == batch
    row_energy = jnp.sum(jnp.where(pick, columns, 0.0), axis=1, keepdims=True)[:64]
    row_energy = jnp.broadcast_to(row_energy - occ_ref[wide], (64, 128))
    row_e[...] = row_energy
    for q in range(8):
        row_exp[pl.ds(q * 64, 64), :] = jnp.exp(-kap_ref[q] * row_energy)

    y_own.wait()
    for d in range(1, ny):
        src_y = lax.rem(y + d, ny)
        y_copy(src_y, src_y).wait_recv()

    def z_copy(p, zz, src_z):
        return pltpu.make_async_remote_copy(
            src_ref=rows.at[zz + p],
            dst_ref=gath.at[batch, p, :, src_z, core],
            send_sem=z_send.at[p, zz],
            recv_sem=z_recv.at[p, src_z],
            device_id=at_wide(y, zz, core),
            device_id_type=MESH,
        )

    z_far_first = sorted(range(1, nz), key=lambda d: -min(d, nz - d))
    z_own = {}
    for p in ORDER:
        for d in z_far_first:
            z_copy(p, lax.rem(zh + d, nz), zh).start()
        z_own[p] = pltpu.make_async_copy(
            rows.at[zh + p], gath.at[batch, p, :, zh, core], local_sem.at[1 + p]
        )
        z_own[p].start()

    half = ny // 2
    parts = {"all": pl.ds(0, ny), "first": pl.ds(0, half), "second": pl.ds(half, ny - half)}

    def g_copy(p, dx, dz, part, slot, to):
        ref = gath.at[at_batch(dx, dz), p, parts[part], :, core]
        return pltpu.make_async_remote_copy(
            src_ref=ref, dst_ref=ref, send_sem=g_send.at[p, slot], recv_sem=g_recv.at[p, slot],
            device_id=to, device_id_type=MESH,
        )

    sends = {
        0: (right, 0, 0, "all"),
        1: (left, 0, 0, "all"),
        2: (over, 0, 0, "all"),
        3: (right, -1, 0, "first"),
        4: (left, 1, 0, "second"),
        5: (right, 0, 1, "all"),
        6: (left, 0, 1, "all"),
        7: (over, 2, 0, "all"),
    }
    gets = {
        0: (-1, 0, "all"),
        1: (1, 0, "all"),
        2: (0, 1, "all"),
        3: (2, 0, "first"),
        4: (2, 0, "second"),
        5: (-1, 1, "all"),
        6: (1, 1, "all"),
        7: (2, 1, "all"),
    }
    blocks = ((0, 0), (-1, 0), (1, 0), (0, 1), (2, 0), (-1, 1), (1, 1), (2, 1))

    def g_start(p, slot):
        to, dx, dz, part = sends[slot]
        g_copy(p, dx, dz, part, slot, to).start()

    def g_wait(p, slot):
        dx, dz, part = gets[slot]
        g_copy(p, dx, dz, part, slot, right).wait_recv()

    def s_copy(p, block, cc):
        dx, dz = blocks[block]
        ref = gath.at[at_batch(dx, dz), p, :, :, cc]
        return pltpu.make_async_remote_copy(
            src_ref=ref, dst_ref=ref, send_sem=s_send.at[p, block], recv_sem=s_recv.at[p, block],
            device_id=sibling, device_id_type=MESH,
        )

    def s_start(p, block):
        s_copy(p, block, core).start()

    def s_wait(p, block):
        s_copy(p, block, 1 - core).wait_recv()

    def flat(b, p):
        return gath.at[b, p].reshape(naux, 128)

    lane = lax.broadcasted_iota(jnp.int32, (1, 128), 1)
    lane_low = lane < 64
    tn = 256 if naux % 256 == 0 else naux

    def compute(p, first_block, second_block, first, last):
        b0 = at_batch(*blocks[first_block])
        b1 = at_batch(*blocks[second_block])
        r0, r1 = flat(b0, p), flat(b1, p)
        pair = lax.rem(own_pair + p - 1 + pairs, pairs)
        occ_j = jnp.where(lane_low, occ_ref[2 * pair], occ_ref[2 * pair + 1])
        offset = 2 * (p - 1) + jnp.where(lane_low, 0, 1) - core
        keep = jnp.logical_and(offset >= -HALF, offset <= HALF)
        for n, (b, r) in enumerate(((b0, r0), (b1, r1))):
            coulomb = jnp.dot(
                tit[pl.ds(pl.multiple_of(core * 64, 64), 64), :], r[...],
                preferred_element_type=jnp.float32,
            )
            col_e = vir2[pl.ds(b, 1), :] - occ_j
            scaled = -coulomb / (row_e[...] + col_e)
            scaled = jnp.where(keep, scaled, 0.0)
            col_exp = jnp.exp(-kvec[...] * col_e)
            for q in range(8):
                damp = 1.0 - row_exp[pl.ds(q * 64, 64), :] * col_exp[q : q + 1, :]
                amp[pl.ds(q * 64, 64), n * 128 : (n + 1) * 128] = (scaled * (damp * damp)).astype(
                    jnp.bfloat16
                )

        def tile(n, carry):
            at = pl.multiple_of(n * tn, tn)
            rhs = jnp.concatenate([r0[pl.ds(at, tn), :], r1[pl.ds(at, tn), :]], axis=1)
            part = lax.dot_general(
                amp[...], rhs, (((1,), (1,)), ((), ())), preferred_element_type=jnp.float32
            )
            if first:
                acc[:, pl.ds(at, tn)] = part
            elif last:
                out_ref[:, pl.ds(at, tn)] = (acc[:, pl.ds(at, tn)] + part).astype(jnp.bfloat16)
            else:
                acc[:, pl.ds(at, tn)] += part
            return carry

        lax.fori_loop(0, naux // tn, tile, 0)

    for p in ORDER:
        z_own[p].wait()
        for d in range(1, nz):
            src_z = lax.rem(zh + d, nz)
            z_copy(p, src_z, src_z).wait_recv()
        for slot in (0, 1, 2):
            g_start(p, slot)
        s_start(p, 0)

    for p in ORDER:
        g_wait(p, 0)
        g_start(p, 3)
        s_start(p, 1)
        g_wait(p, 1)
        g_start(p, 4)
        s_start(p, 2)
        g_wait(p, 2)
        g_start(p, 5)
        g_start(p, 6)
        s_start(p, 3)
        for block in range(4):
            s_wait(p, block)
        if p == ORDER[0]:
            tit[...] = jnp.transpose(flat(batch, 1)[...])
        compute(p, 0, 3, p == ORDER[0], False)
        compute(p, 1, 2, False, False)
    for p in ORDER:
        g_wait(p, 3)
        g_wait(p, 4)
        g_start(p, 7)
        s_start(p, 4)
        g_wait(p, 5)
        s_start(p, 5)
        g_wait(p, 6)
        s_start(p, 6)
        g_wait(p, 7)
        s_start(p, 7)
        for block in range(4, 8):
            s_wait(p, block)
        compute(p, 4, 7, False, False)
        compute(p, 5, 6, False, p == ORDER[2])

    for d in range(1, ny):
        y_copy(lax.rem(y + d, ny), y).wait_send()
    for p in range(3):
        for d in range(1, nz):
            z_copy(p, lax.rem(zh + d, nz), zh).wait_send()
        for slot in range(8):
            to, dx, dz, part = sends[slot]
            g_copy(p, dx, dz, part, slot, to).wait_send()
        for block in range(8):
            s_copy(p, block, core).wait_send()


def on_device(ny, nz, integrals, vir_coeff, occ_energy, vir_energy, kappas):
    aux_local, nocc, basis = integrals.shape
    naux = aux_local * ny * nz * 2
    pairs = ny * nz
    vmem = pl.BlockSpec(memory_space=pltpu.VMEM)
    smem = pl.BlockSpec(memory_space=pltpu.SMEM)
    sub = aux_local // 8
    bf16, f32 = jnp.bfloat16, jnp.float32
    dma = pltpu.SemaphoreType.DMA
    out = pl.pallas_call(
        functools.partial(kernel, ny, nz),
        out_shape=jax.ShapeDtypeStruct((8 * 64, naux), bf16),
        in_specs=[vmem, vmem, vmem, smem, smem],
        out_specs=vmem,
        scratch_shapes=[
            pltpu.VMEM((aux_local * nocc, 128), f32),
            pltpu.VMEM((pairs + 2, sub, 8, 128), bf16),
            pltpu.VMEM((nz + 2, ny, sub, 8, 128), bf16),
            pltpu.VMEM((2 * NX, 3, ny, nz, 2, sub, 8, 128), bf16),
            pltpu.VMEM((128, naux), bf16),
            pltpu.VMEM((512, 128), f32),
            pltpu.VMEM((8, 128), f32),
            pltpu.VMEM((8, 128), f32),
            pltpu.VMEM((64, 128), f32),
            pltpu.VMEM((512, 256), bf16),
            pltpu.VMEM((512, naux), f32),
            dma((4,)),
            dma((ny,)),
            dma((ny,)),
            dma((3, nz)),
            dma((3, nz)),
            dma((3, 8)),
            dma((3, 8)),
            dma((3, 8)),
            dma((3, 8)),
        ],
        compiler_params=pltpu.CompilerParams(
            collective_id=0, has_side_effects=True, vmem_limit_bytes=60 * 1024 * 1024
        ),
    )(
        integrals.reshape(aux_local * nocc, basis), vir_coeff, vir_energy.reshape(1, -1),
        occ_energy, kappas,
    )
    return out.reshape(8, 1, 64, naux)


def solution(mesh):
    wide = mesh.shape["wide"]
    nz = 4 if wide == 64 else 2
    ny = wide // (2 * nz)
    return jax.shard_map(
        functools.partial(on_device, ny, nz),
        mesh=mesh,
        in_specs=(P("wide", None, None), P(None, "batch"), P(), P(), P()),
        out_specs=P(None, "wide", "batch", None),
        check_vma=False,
    )
```

time: 346 us -> 99.5 us (0.29)
  the two profiles are of different devices: /device:TPU:31 before, /device:TPU:1 now
where the time goes in v1:
time: 99.5 us; the launch traced here: 99.3 us
  Pallas kernels  95 us (95%)
  local copies, waits for them, and re-layouts  4.34 us (4%)
    pallas_call x1, Pallas kernels, on_device(): pl.pallas_call(functools.partial(kernel, ny, nz), out_shape=jax.ShapeDtyp...  95 us
    unnamed x2, local copies, waits for them, and re-layouts  4.34 us

profile of v1, /device:TPU:1, one launch (start us, length us, event | category | flops | bytes accessed | tf_op | source)
XLA Modules:
  0.0 99.3 jit_solution(9997666121192652089)
XLA Ops:
  0.0 1.7 %copy.6.coef_ref = bf16[640,64]{1,0:T(8,128)(2,1)} copy(bf16[640,64]{0,1:T(8,128)(2,1)} %param.6) | data formatting | bytes 163840 | tf_op args[1]
  1.7 95.0 %shard_map.55 = bf16[512,1536]{1,0:T(8,128)(2,1)} custom-call(bf16[1536,640]{1,0:T(8,128)(2,1)} %bitcast.6, bf16[640,64]{1,0:T(8,128)(2,1)} %copy.6.coef_ref, f32[1,512]{1,0:T(1,128)} %bitcast.7, f32[64]{0:T(128)} %occ_ref.1, f32[8]{0:T(128)} %kap_ref.1), custom_call_target="tpu_custom_call" | custom-call | tf_op jit(solution)/shard_map/pallas_call | solution.py:298
  96.7 2.7 %copy.9 = bf16[8,1,64,1536]{3,2,1,0:T(8,128)(2,1)} copy(bf16[8,1,64,1536]{3,2,1,0:T(8,128)(2,1)} %bitcast.5) | data formatting | bytes 3145728

commit v2 on v1

--- a/solution.py
+++ b/solution.py
@@ -10,13 +10,12 @@
 HALF = 2
 NX = 4
 MESH = pl.DeviceIdType.MESH
-ORDER = (1, 0, 2)
 
 
 def kernel(
     ny, nz, ints_ref, coef_ref, vir_ref, occ_ref, kap_ref, out_ref,
-    full, mine, rows, gath, tit, row_exp, vir2, kvec, row_e, amp, acc,
-    local_sem, y_send, y_recv, z_send, z_recv, g_send, g_recv, s_send, s_recv,
+    ints, full, mine, rows, gath, tit, row_exp, vir2, kvec, row_e, amp, acc,
+    in_sem, local_sem, y_send, y_recv, z_send, z_recv, g_send, g_recv, s_send, s_recv,
 ):
     wide = lax.axis_index("wide")
     batch = lax.axis_index("batch")
@@ -41,6 +40,16 @@
     sibling = at_wide(y, zh, 1 - core)
     left, right, over = dev_batch(-1, 0), dev_batch(1, 0), dev_batch(0, 1)
 
+    steps = in_sem.shape[0]
+    tall = full.shape[0] // steps
+
+    def fetch(k):
+        part = pl.ds(k * tall, tall)
+        return pltpu.make_async_copy(ints_ref.at[part], ints.at[part], in_sem.at[k])
+
+    for k in range(steps):
+        fetch(k).start()
+
     barrier = pltpu.get_barrier_semaphore()
     peers = [at_wide(lax.rem(y + d, ny), zh, core) for d in range(1, ny)]
     peers += [at_wide(y, lax.rem(zh + d, nz), core) for d in range(1, nz)]
@@ -48,18 +57,13 @@
     for peer in peers:
         pl.semaphore_signal(barrier, inc=1, device_id=peer, device_id_type=MESH)
 
-    coef2 = jnp.concatenate([coef_ref[...], coef_ref[...]], axis=1)
-    steps = 4
-    tall = full.shape[0] // steps
-
-    def transform(s, carry):
-        at = pl.multiple_of(s * tall, tall)
-        full[pl.ds(at, tall), :] = jnp.dot(
-            ints_ref[pl.ds(at, tall), :], coef2, preferred_element_type=jnp.float32
-        )
-        return carry
-
-    lax.fori_loop(0, steps, transform, 0)
+    coef2 = jnp.concatenate([coef_ref[...], coef_ref[...]], axis=0)
+    for k in range(steps):
+        fetch(k).wait()
+        full[pl.ds(k * tall, tall), :] = lax.dot_general(
+            ints[pl.ds(k * tall, tall), :], coef2, (((1,), (1,)), ((), ())),
+            preferred_element_type=jnp.float32,
+        )
     nocc = 2 * pairs
     nrow = full.shape[0] // nocc
     low = lax.broadcasted_iota(jnp.int32, (nrow, 128), 1) < 64
@@ -75,19 +79,23 @@
 
     pl.semaphore_wait(barrier, len(peers))
 
-    def y_copy(yy, src_y):
+    y_parts = ((1, nz), (0, 1), (nz + 1, 1))
+
+    def y_copy(part, yy, src_y):
+        at, count = y_parts[part]
         return pltpu.make_async_remote_copy(
-            src_ref=mine.at[pl.ds(nz * yy, nz + 2)],
-            dst_ref=rows.at[:, src_y],
-            send_sem=y_send.at[yy],
-            recv_sem=y_recv.at[src_y],
+            src_ref=mine.at[pl.ds(nz * yy + at, count)],
+            dst_ref=rows.at[pl.ds(at, count), src_y],
+            send_sem=y_send.at[part, yy],
+            recv_sem=y_recv.at[part, src_y],
             device_id=at_wide(yy, zh, core),
             device_id_type=MESH,
         )
 
     far_first = sorted(range(1, ny), key=lambda d: -min(d, ny - d))
-    for d in far_first:
-        y_copy(lax.rem(y + d, ny), y).start()
+    for part in range(3):
+        for d in far_first:
+            y_copy(part, lax.rem(y + d, ny), y).start()
     y_own = pltpu.make_async_copy(mine.at[pl.ds(nz * y, nz + 2)], rows.at[:, y], local_sem.at[0])
     y_own.start()
 
@@ -108,9 +116,11 @@
         row_exp[pl.ds(q * 64, 64), :] = jnp.exp(-kap_ref[q] * row_energy)
 
     y_own.wait()
-    for d in range(1, ny):
-        src_y = lax.rem(y + d, ny)
-        y_copy(src_y, src_y).wait_recv()
+
+    def y_wait(part):
+        for d in range(1, ny):
+            src_y = lax.rem(y + d, ny)
+            y_copy(part, src_y, src_y).wait_recv()
 
     def z_copy(p, zz, src_z):
         return pltpu.make_async_remote_copy(
@@ -123,14 +133,22 @@
         )
 
     z_far_first = sorted(range(1, nz), key=lambda d: -min(d, nz - d))
-    z_own = {}
-    for p in ORDER:
+
+    def z_own(p):
+        return pltpu.make_async_copy(
+            rows.at[zh + p], gath.at[batch, p, :, zh, core], local_sem.at[1 + p]
+        )
+
+    def z_start(p):
         for d in z_far_first:
             z_copy(p, lax.rem(zh + d, nz), zh).start()
-        z_own[p] = pltpu.make_async_copy(
-            rows.at[zh + p], gath.at[batch, p, :, zh, core], local_sem.at[1 + p]
-        )
-        z_own[p].start()
+        z_own(p).start()
+
+    def z_wait(p):
+        z_own(p).wait()
+        for d in range(1, nz):
+            src_z = lax.rem(zh + d, nz)
+            z_copy(p, src_z, src_z).wait_recv()
 
     half = ny // 2
     parts = {"all": pl.ds(0, ny), "first": pl.ds(0, half), "second": pl.ds(half, ny - half)}
@@ -232,16 +250,13 @@
 
         lax.fori_loop(0, naux // tn, tile, 0)
 
-    for p in ORDER:
-        z_own[p].wait()
-        for d in range(1, nz):
-            src_z = lax.rem(zh + d, nz)
-            z_copy(p, src_z, src_z).wait_recv()
+    def own(p):
+        z_wait(p)
         for slot in (0, 1, 2):
             g_start(p, slot)
         s_start(p, 0)
 
-    for p in ORDER:
+    def near(p):
         g_wait(p, 0)
         g_start(p, 3)
         s_start(p, 1)
@@ -252,30 +267,62 @@
         g_start(p, 5)
         g_start(p, 6)
         s_start(p, 3)
-        for block in range(4):
-            s_wait(p, block)
-        if p == ORDER[0]:
-            tit[...] = jnp.transpose(flat(batch, 1)[...])
-        compute(p, 0, 3, p == ORDER[0], False)
-        compute(p, 1, 2, False, False)
-    for p in ORDER:
+
+    def opposite(p):
         g_wait(p, 3)
         g_wait(p, 4)
         g_start(p, 7)
         s_start(p, 4)
-        g_wait(p, 5)
-        s_start(p, 5)
-        g_wait(p, 6)
-        s_start(p, 6)
-        g_wait(p, 7)
-        s_start(p, 7)
-        for block in range(4, 8):
+
+    def last_of(p):
+        for slot, block in ((5, 5), (6, 6), (7, 7)):
+            g_wait(p, slot)
+            s_start(p, block)
+
+    def shared(p, *which):
+        for block in which:
             s_wait(p, block)
-        compute(p, 4, 7, False, False)
-        compute(p, 5, 6, False, p == ORDER[2])
-
-    for d in range(1, ny):
-        y_copy(lax.rem(y + d, ny), y).wait_send()
+
+    def near_compute(p):
+        shared(p, 0, 1, 2, 3)
+        if p == 1:
+            tit[...] = jnp.transpose(flat(batch, 1)[...])
+        compute(p, 0, 3, p == 1, False)
+        compute(p, 1, 2, False, False)
+
+    def far_compute(p):
+        shared(p, 4, 5, 6, 7)
+        compute(p, 5, 6, False, False)
+        compute(p, 4, 7, False, p == 2)
+
+    y_wait(0)
+    z_start(1)
+    y_wait(1)
+    y_wait(2)
+    z_start(0)
+    z_start(2)
+    own(1)
+    own(0)
+    near(1)
+    near_compute(1)
+    own(2)
+    near(0)
+    near_compute(0)
+    opposite(1)
+    near(2)
+    near_compute(2)
+    opposite(0)
+    last_of(1)
+    far_compute(1)
+    opposite(2)
+    last_of(0)
+    far_compute(0)
+    last_of(2)
+    far_compute(2)
+
+    for part in range(3):
+        for d in range(1, ny):
+            y_copy(part, lax.rem(y + d, ny), y).wait_send()
     for p in range(3):
         for d in range(1, nz):
             z_copy(p, lax.rem(zh + d, nz), zh).wait_send()
@@ -297,10 +344,11 @@
     dma = pltpu.SemaphoreType.DMA
     out = pl.pallas_call(
         functools.partial(kernel, ny, nz),
-        out_shape=jax.ShapeDtypeStruct((8 * 64, naux), bf16),
-        in_specs=[vmem, vmem, vmem, smem, smem],
+        out_shape=pltpu.VMEM((8 * 64, naux), bf16),
+        in_specs=[pl.BlockSpec(memory_space=pl.ANY), vmem, vmem, smem, smem],
         out_specs=vmem,
         scratch_shapes=[
+            pltpu.VMEM((aux_local * nocc, basis), bf16),
             pltpu.VMEM((aux_local * nocc, 128), f32),
             pltpu.VMEM((pairs + 2, sub, 8, 128), bf16),
             pltpu.VMEM((nz + 2, ny, sub, 8, 128), bf16),
@@ -313,8 +361,9 @@
             pltpu.VMEM((512, 256), bf16),
             pltpu.VMEM((512, naux), f32),
             dma((4,)),
-            dma((ny,)),
-            dma((ny,)),
+            dma((4,)),
+            dma((3, ny)),
+            dma((3, ny)),
             dma((3, nz)),
             dma((3, nz)),
             dma((3, 8)),
@@ -326,7 +375,7 @@
             collective_id=0, has_side_effects=True, vmem_limit_bytes=60 * 1024 * 1024
         ),
     )(
-        integrals.reshape(aux_local * nocc, basis), vir_coeff, vir_energy.reshape(1, -1),
+        integrals.reshape(aux_local * nocc, basis), vir_coeff.T, vir_energy.reshape(1, -1),
         occ_energy, kappas,
     )
     return out.reshape(8, 1, 64, naux)

time: 99.5 us -> 79.4 us (0.80)
  the two profiles are of different devices: /device:TPU:1 before, /device:TPU:25 now
where the time goes in v2:
time: 79.4 us; the launch traced here: 79.2 us
  Pallas kernels  78.1 us (98%)
  local copies, waits for them, and re-layouts  1.15 us (1%)
    pallas_call x1, Pallas kernels, on_device(): pl.pallas_call(functools.partial(kernel, ny, nz), out_shape=pltpu.VMEM((8...  78.1 us

profile of v2, /device:TPU:25, one launch (start us, length us, event | category | flops | bytes accessed | tf_op | source)
XLA Modules:
  0.0 79.2 jit_solution(5212708206268634571)
XLA Ops:
  0.0 78.1 %shard_map.55 = bf16[512,1536]{1,0:T(8,128)(2,1)S(1)} custom-call(bf16[1536,640]{1,0:T(8,128)(2,1)} %bitcast.7, bf16[64,640]{1,0:T(8,128)(2,1)} %bitcast.8, f32[1,512]{1,0:T(1,128)} %bitcast.9, f32[64]{0:T(128)} %occ_ref.1, f32[8]{0:T(128)} %kap_ref.1), custom_call_target="tpu_custom_call" | custom-call | tf_op jit(solution)/shard_map/pallas_call | solution.py:345
  78.1 1.1 %copy.8 = bf16[8,1,64,1536]{3,2,1,0:T(8,128)(2,1)} copy(bf16[8,1,64,1536]{3,2,1,0:T(8,128)(2,1)S(1)} %bitcast.6) | data formatting | bytes 3145728

commit v3 on v2

--- a/solution.py
+++ b/solution.py
@@ -14,8 +14,8 @@
 
 def kernel(
     ny, nz, ints_ref, coef_ref, vir_ref, occ_ref, kap_ref, out_ref,
-    ints, full, mine, rows, gath, tit, row_exp, vir2, kvec, row_e, amp, acc,
-    in_sem, local_sem, y_send, y_recv, z_send, z_recv, g_send, g_recv, s_send, s_recv,
+    ints, full, mine, gath, tit, row_exp, vir2, kvec, row_e, amp, acc,
+    in_sem, a_send, a_recv, g_send, g_recv, s_send, s_recv,
 ):
     wide = lax.axis_index("wide")
     batch = lax.axis_index("batch")
@@ -51,8 +51,12 @@
         fetch(k).start()
 
     barrier = pltpu.get_barrier_semaphore()
-    peers = [at_wide(lax.rem(y + d, ny), zh, core) for d in range(1, ny)]
-    peers += [at_wide(y, lax.rem(zh + d, nz), core) for d in range(1, nz)]
+    far = sorted(
+        ((dy, dz) for dy in range(ny) for dz in range(nz) if (dy, dz) != (0, 0)),
+        key=lambda d: -min(d[0], ny - d[0]) - 2 * min(d[1], nz - d[1]),
+    )
+    owners = [(lax.rem(y + dy, ny), lax.rem(zh + dz, nz)) for dy, dz in far]
+    peers = [at_wide(yy, zz, core) for yy, zz in owners]
     peers += [left, right, over, sibling]
     for peer in peers:
         pl.semaphore_signal(barrier, inc=1, device_id=peer, device_id_type=MESH)
@@ -79,25 +83,26 @@
 
     pl.semaphore_wait(barrier, len(peers))
 
-    y_parts = ((1, nz), (0, 1), (nz + 1, 1))
-
-    def y_copy(part, yy, src_y):
-        at, count = y_parts[part]
+    def a_copy(p, yy, zz):
         return pltpu.make_async_remote_copy(
-            src_ref=mine.at[pl.ds(nz * yy + at, count)],
-            dst_ref=rows.at[pl.ds(at, count), src_y],
-            send_sem=y_send.at[part, yy],
-            recv_sem=y_recv.at[part, src_y],
-            device_id=at_wide(yy, zh, core),
+            src_ref=mine.at[yy * nz + zz + p],
+            dst_ref=gath.at[batch, p, y, zh, core],
+            send_sem=a_send.at[p],
+            recv_sem=a_recv.at[p],
+            device_id=at_wide(yy, zz, core),
             device_id_type=MESH,
         )
 
-    far_first = sorted(range(1, ny), key=lambda d: -min(d, ny - d))
-    for part in range(3):
-        for d in far_first:
-            y_copy(part, lax.rem(y + d, ny), y).start()
-    y_own = pltpu.make_async_copy(mine.at[pl.ds(nz * y, nz + 2)], rows.at[:, y], local_sem.at[0])
-    y_own.start()
+    for p in (1, 0, 2):
+        pltpu.make_async_copy(
+            mine.at[own_pair + p], gath.at[batch, p, y, zh, core], a_recv.at[p]
+        ).start()
+        for yy, zz in owners:
+            a_copy(p, yy, zz).start()
+
+    def a_wait(p):
+        ref = gath.at[batch, p, :, :, core]
+        pltpu.make_async_copy(ref, ref, a_recv.at[p]).wait()
 
     for b in range(2 * NX):
         part = vir_ref[:, b * 64 : (b + 1) * 64]
@@ -114,41 +119,6 @@
     row_e[...] = row_energy
     for q in range(8):
         row_exp[pl.ds(q * 64, 64), :] = jnp.exp(-kap_ref[q] * row_energy)
-
-    y_own.wait()
-
-    def y_wait(part):
-        for d in range(1, ny):
-            src_y = lax.rem(y + d, ny)
-            y_copy(part, src_y, src_y).wait_recv()
-
-    def z_copy(p, zz, src_z):
-        return pltpu.make_async_remote_copy(
-            src_ref=rows.at[zz + p],
-            dst_ref=gath.at[batch, p, :, src_z, core],
-            send_sem=z_send.at[p, zz],
-            recv_sem=z_recv.at[p, src_z],
-            device_id=at_wide(y, zz, core),
-            device_id_type=MESH,
-        )
-
-    z_far_first = sorted(range(1, nz), key=lambda d: -min(d, nz - d))
-
-    def z_own(p):
-        return pltpu.make_async_copy(
-            rows.at[zh + p], gath.at[batch, p, :, zh, core], local_sem.at[1 + p]
-        )
-
-    def z_start(p):
-        for d in z_far_first:
-            z_copy(p, lax.rem(zh + d, nz), zh).start()
-        z_own(p).start()
-
-    def z_wait(p):
-        z_own(p).wait()
-        for d in range(1, nz):
-            src_z = lax.rem(zh + d, nz)
-            z_copy(p, src_z, src_z).wait_recv()
 
     half = ny // 2
     parts = {"all": pl.ds(0, ny), "first": pl.ds(0, half), "second": pl.ds(half, ny - half)}
@@ -251,7 +221,7 @@
         lax.fori_loop(0, naux // tn, tile, 0)
 
     def own(p):
-        z_wait(p)
+        a_wait(p)
         for slot in (0, 1, 2):
             g_start(p, slot)
         s_start(p, 0)
@@ -295,12 +265,6 @@
         compute(p, 5, 6, False, False)
         compute(p, 4, 7, False, p == 2)
 
-    y_wait(0)
-    z_start(1)
-    y_wait(1)
-    y_wait(2)
-    z_start(0)
-    z_start(2)
     own(1)
     own(0)
     near(1)
@@ -320,12 +284,9 @@
     last_of(2)
     far_compute(2)
 
-    for part in range(3):
-        for d in range(1, ny):
-            y_copy(part, lax.rem(y + d, ny), y).wait_send()
     for p in range(3):
-        for d in range(1, nz):
-            z_copy(p, lax.rem(zh + d, nz), zh).wait_send()
+        sent = mine.at[pl.ds(0, pairs - 1)]
+        pltpu.make_async_copy(sent, sent, a_send.at[p]).wait()
         for slot in range(8):
             to, dx, dz, part = sends[slot]
             g_copy(p, dx, dz, part, slot, to).wait_send()
@@ -351,7 +312,6 @@
             pltpu.VMEM((aux_local * nocc, basis), bf16),
             pltpu.VMEM((aux_local * nocc, 128), f32),
             pltpu.VMEM((pairs + 2, sub, 8, 128), bf16),
-            pltpu.VMEM((nz + 2, ny, sub, 8, 128), bf16),
             pltpu.VMEM((2 * NX, 3, ny, nz, 2, sub, 8, 128), bf16),
             pltpu.VMEM((128, naux), bf16),
             pltpu.VMEM((512, 128), f32),
@@ -361,11 +321,8 @@
             pltpu.VMEM((512, 256), bf16),
             pltpu.VMEM((512, naux), f32),
             dma((4,)),
-            dma((4,)),
-            dma((3, ny)),
-            dma((3, ny)),
-            dma((3, nz)),
-            dma((3, nz)),
+            dma((3,)),
+            dma((3,)),
             dma((3, 8)),
             dma((3, 8)),
             dma((3, 8)),

time: 79.4 us -> 75 us (0.945)
  the two profiles are of different devices: /device:TPU:25 before, /device:TPU:1 now
where the time goes in v3:
time: 75 us; the launch traced here: 74.8 us
  Pallas kernels  73.7 us (98%)
  local copies, waits for them, and re-layouts  1.15 us (2%)
    pallas_call x1, Pallas kernels, on_device(): pl.pallas_call(functools.partial(kernel, ny, nz), out_shape=pltpu.VMEM((8...  73.7 us

profile of v3, /device:TPU:1, one launch (start us, length us, event | category | flops | bytes accessed | tf_op | source)
XLA Modules:
  0.0 74.8 jit_solution(13541260653031902443)
XLA Ops:
  0.0 73.7 %shard_map.55 = bf16[512,1536]{1,0:T(8,128)(2,1)S(1)} custom-call(bf16[1536,640]{1,0:T(8,128)(2,1)} %bitcast.7, bf16[64,640]{1,0:T(8,128)(2,1)} %bitcast.8, f32[1,512]{1,0:T(1,128)} %bitcast.9, f32[64]{0:T(128)} %occ_ref.1, f32[8]{0:T(128)} %kap_ref.1), custom_call_target="tpu_custom_call" | custom-call | tf_op jit(solution)/shard_map/pallas_call | solution.py:306
  73.7 1.1 %copy.8 = bf16[8,1,64,1536]{3,2,1,0:T(8,128)(2,1)} copy(bf16[8,1,64,1536]{3,2,1,0:T(8,128)(2,1)S(1)} %bitcast.6) | data formatting | bytes 3145728

commit v4 on v3

--- a/solution.py
+++ b/solution.py
@@ -8,13 +8,15 @@
 from jax.sharding import PartitionSpec as P
 
 HALF = 2
+UNROLL = True
+TN = 256
 NX = 4
 MESH = pl.DeviceIdType.MESH
 
 
 def kernel(
-    ny, nz, ints_ref, coef_ref, vir_ref, occ_ref, kap_ref, out_ref,
-    ints, full, mine, gath, tit, row_exp, vir2, kvec, row_e, amp, acc,
+    ny, nz, ints_in, coef_in, vir_in, occ_in, kap_in, out_ref,
+    ints, coef_ref, vir_ref, occ_ref, kap_ref, full, mine, gath, tit, row_exp, vir2, kvec, row_e, amp, acc,
     in_sem, a_send, a_recv, g_send, g_recv, s_send, s_recv,
 ):
     wide = lax.axis_index("wide")
@@ -40,16 +42,6 @@
     sibling = at_wide(y, zh, 1 - core)
     left, right, over = dev_batch(-1, 0), dev_batch(1, 0), dev_batch(0, 1)
 
-    steps = in_sem.shape[0]
-    tall = full.shape[0] // steps
-
-    def fetch(k):
-        part = pl.ds(k * tall, tall)
-        return pltpu.make_async_copy(ints_ref.at[part], ints.at[part], in_sem.at[k])
-
-    for k in range(steps):
-        fetch(k).start()
-
     barrier = pltpu.get_barrier_semaphore()
     far = sorted(
         ((dy, dz) for dy in range(ny) for dz in range(nz) if (dy, dz) != (0, 0)),
@@ -61,6 +53,25 @@
     for peer in peers:
         pl.semaphore_signal(barrier, inc=1, device_id=peer, device_id_type=MESH)
 
+    steps = 4
+    tall = full.shape[0] // steps
+
+    def fetch(k):
+        part = pl.ds(k * tall, tall)
+        return pltpu.make_async_copy(ints_in.at[part], ints.at[part], in_sem.at[k])
+
+    small = [
+        pltpu.make_async_copy(src, dst, in_sem.at[steps + k])
+        for k, (src, dst) in enumerate(
+            ((coef_in, coef_ref), (vir_in, vir_ref), (occ_in, occ_ref), (kap_in, kap_ref))
+        )
+    ]
+    small[0].start()
+    for k in range(steps):
+        fetch(k).start()
+    for copy in small[1:]:
+        copy.start()
+    small[0].wait()
     coef2 = jnp.concatenate([coef_ref[...], coef_ref[...]], axis=0)
     for k in range(steps):
         fetch(k).wait()
@@ -104,6 +115,8 @@
         ref = gath.at[batch, p, :, :, core]
         pltpu.make_async_copy(ref, ref, a_recv.at[p]).wait()
 
+    for copy in small[1:]:
+        copy.wait()
     for b in range(2 * NX):
         part = vir_ref[:, b * 64 : (b + 1) * 64]
         vir2[pl.ds(b, 1), :] = jnp.concatenate([part, part], axis=1)
@@ -179,7 +192,7 @@
 
     lane = lax.broadcasted_iota(jnp.int32, (1, 128), 1)
     lane_low = lane < 64
-    tn = 256 if naux % 256 == 0 else naux
+    tn = TN if naux % TN == 0 else naux
 
     def compute(p, first_block, second_block, first, last):
         b0 = at_batch(*blocks[first_block])
@@ -189,23 +202,23 @@
         occ_j = jnp.where(lane_low, occ_ref[2 * pair], occ_ref[2 * pair + 1])
         offset = 2 * (p - 1) + jnp.where(lane_low, 0, 1) - core
         keep = jnp.logical_and(offset >= -HALF, offset <= HALF)
-        for n, (b, r) in enumerate(((b0, r0), (b1, r1))):
-            coulomb = jnp.dot(
-                tit[pl.ds(pl.multiple_of(core * 64, 64), 64), :], r[...],
-                preferred_element_type=jnp.float32,
-            )
-            col_e = vir2[pl.ds(b, 1), :] - occ_j
-            scaled = -coulomb / (row_e[...] + col_e)
-            scaled = jnp.where(keep, scaled, 0.0)
-            col_exp = jnp.exp(-kvec[...] * col_e)
-            for q in range(8):
-                damp = 1.0 - row_exp[pl.ds(q * 64, 64), :] * col_exp[q : q + 1, :]
-                amp[pl.ds(q * 64, 64), n * 128 : (n + 1) * 128] = (scaled * (damp * damp)).astype(
-                    jnp.bfloat16
-                )
+        col_e = jnp.concatenate([vir2[pl.ds(b, 1), :] - occ_j for b in (b0, b1)], axis=1)
+        coulomb = jnp.dot(
+            tit[pl.ds(pl.multiple_of(core * 64, 64), 64), :],
+            jnp.concatenate([r0[...], r1[...]], axis=1),
+            preferred_element_type=jnp.float32,
+        )
+        rows_e = jnp.concatenate([row_e[...]] * 2, axis=1)
+        scaled = -coulomb / (rows_e + col_e)
+        scaled = jnp.where(jnp.concatenate([keep] * 2, axis=1), scaled, 0.0)
+        col_exp = jnp.exp(-jnp.concatenate([kvec[...]] * 2, axis=1) * col_e)
+        for q in range(8):
+            grown = row_exp[pl.ds(q * 64, 64), :]
+            damp = 1.0 - jnp.concatenate([grown] * 2, axis=1) * col_exp[q : q + 1, :]
+            amp[pl.ds(q * 64, 64), :] = (scaled * (damp * damp)).astype(jnp.bfloat16)
 
         def tile(n, carry):
-            at = pl.multiple_of(n * tn, tn)
+            at = n * tn if isinstance(n, int) else pl.multiple_of(n * tn, tn)
             rhs = jnp.concatenate([r0[pl.ds(at, tn), :], r1[pl.ds(at, tn), :]], axis=1)
             part = lax.dot_general(
                 amp[...], rhs, (((1,), (1,)), ((), ())), preferred_element_type=jnp.float32
@@ -218,7 +231,11 @@
                 acc[:, pl.ds(at, tn)] += part
             return carry
 
-        lax.fori_loop(0, naux // tn, tile, 0)
+        if UNROLL:
+            for n in range(naux // tn):
+                tile(n, 0)
+        else:
+            lax.fori_loop(0, naux // tn, tile, 0)
 
     def own(p):
         a_wait(p)
@@ -233,6 +250,8 @@
         g_wait(p, 1)
         g_start(p, 4)
         s_start(p, 2)
+
+    def across(p):
         g_wait(p, 2)
         g_start(p, 5)
         g_start(p, 6)
@@ -244,45 +263,58 @@
         g_start(p, 7)
         s_start(p, 4)
 
-    def last_of(p):
-        for slot, block in ((5, 5), (6, 6), (7, 7)):
+    def corners(p):
+        for slot, block in ((5, 5), (6, 6)):
             g_wait(p, slot)
             s_start(p, block)
 
-    def shared(p, *which):
-        for block in which:
+    def far_corner(p):
+        g_wait(p, 7)
+        s_start(p, 7)
+
+    def step(p, first_block, second_block, first=False, last=False):
+        for block in (first_block, second_block):
             s_wait(p, block)
-
-    def near_compute(p):
-        shared(p, 0, 1, 2, 3)
-        if p == 1:
-            tit[...] = jnp.transpose(flat(batch, 1)[...])
-        compute(p, 0, 3, p == 1, False)
-        compute(p, 1, 2, False, False)
-
-    def far_compute(p):
-        shared(p, 4, 5, 6, 7)
-        compute(p, 5, 6, False, False)
-        compute(p, 4, 7, False, p == 2)
+        compute(p, first_block, second_block, first, last)
+
+    def compute_own(p):
+        if p != 1:
+            s_wait(p, 0)
+        s_wait(p, 3)
+        compute(p, 0, 3, False, False)
 
     own(1)
     own(0)
     near(1)
-    near_compute(1)
     own(2)
+    s_wait(1, 0)
+    tit[...] = jnp.transpose(flat(batch, 1)[...])
+    step(1, 1, 2, first=True)
     near(0)
-    near_compute(0)
+    step(0, 1, 2)
+    near(2)
+    across(1)
+    compute_own(1)
     opposite(1)
-    near(2)
-    near_compute(2)
+    step(2, 1, 2)
+    across(0)
+    compute_own(0)
+    corners(1)
     opposite(0)
-    last_of(1)
-    far_compute(1)
+    across(2)
+    step(1, 5, 6)
+    compute_own(2)
+    far_corner(1)
+    step(1, 4, 7)
+    corners(0)
     opposite(2)
-    last_of(0)
-    far_compute(0)
-    last_of(2)
-    far_compute(2)
+    step(0, 5, 6)
+    far_corner(0)
+    step(0, 4, 7)
+    corners(2)
+    step(2, 5, 6)
+    far_corner(2)
+    step(2, 4, 7, last=True)
 
     for p in range(3):
         sent = mine.at[pl.ds(0, pairs - 1)]
@@ -299,17 +331,20 @@
     naux = aux_local * ny * nz * 2
     pairs = ny * nz
     vmem = pl.BlockSpec(memory_space=pltpu.VMEM)
-    smem = pl.BlockSpec(memory_space=pltpu.SMEM)
     sub = aux_local // 8
     bf16, f32 = jnp.bfloat16, jnp.float32
     dma = pltpu.SemaphoreType.DMA
     out = pl.pallas_call(
         functools.partial(kernel, ny, nz),
         out_shape=pltpu.VMEM((8 * 64, naux), bf16),
-        in_specs=[pl.BlockSpec(memory_space=pl.ANY), vmem, vmem, smem, smem],
+        in_specs=[pl.BlockSpec(memory_space=pl.ANY)] * 5,
         out_specs=vmem,
         scratch_shapes=[
             pltpu.VMEM((aux_local * nocc, basis), bf16),
+            pltpu.VMEM((64, basis), bf16),
+            pltpu.VMEM((1, 2 * NX * 64), f32),
+            pltpu.SMEM((nocc,), f32),
+            pltpu.SMEM((8,), f32),
             pltpu.VMEM((aux_local * nocc, 128), f32),
             pltpu.VMEM((pairs + 2, sub, 8, 128), bf16),
             pltpu.VMEM((2 * NX, 3, ny, nz, 2, sub, 8, 128), bf16),
@@ -320,7 +355,7 @@
             pltpu.VMEM((64, 128), f32),
             pltpu.VMEM((512, 256), bf16),
             pltpu.VMEM((512, naux), f32),
-            dma((4,)),
+            dma((8,)),
             dma((3,)),
             dma((3,)),
             dma((3, 8)),

time: 75 us -> 69.8 us (0.931)
  Pallas kernels: 73.7 us -> 68.5 us
    pallas_call x1, Pallas kernels: 73.7 us -> 68.5 us  [on_device(): pl.pallas_call(functools.partial(kernel, ny, nz), out_shape=pltpu.VMEM((8...]
where the time goes in v4:
time: 69.8 us; the launch traced here: 69.7 us
  Pallas kernels  68.5 us (98%)
  local copies, waits for them, and re-layouts  1.15 us (2%)
    pallas_call x1, Pallas kernels, on_device(): pl.pallas_call(functools.partial(kernel, ny, nz), out_shape=pltpu.VMEM((8...  68.5 us

profile of v4, /device:TPU:1, one launch (start us, length us, event | category | flops | bytes accessed | tf_op | source)
XLA Modules:
  0.0 69.7 jit_solution(5719395083181430706)
XLA Ops:
  0.0 68.5 %shard_map.55 = bf16[512,1536]{1,0:T(8,128)(2,1)S(1)} custom-call(bf16[1536,640]{1,0:T(8,128)(2,1)} %bitcast.7, bf16[64,640]{1,0:T(8,128)(2,1)} %bitcast.8, f32[1,512]{1,0:T(1,128)} %bitcast.9, f32[64]{0:T(128)} %occ_in.1, f32[8]{0:T(128)} %kap_in.1), custom_call_target="tpu_custom_call" | custom-call | tf_op jit(solution)/shard_map/pallas_call | solution.py:337
  68.5 1.1 %copy.8 = bf16[8,1,64,1536]{3,2,1,0:T(8,128)(2,1)} copy(bf16[8,1,64,1536]{3,2,1,0:T(8,128)(2,1)S(1)} %bitcast.6) | data formatting | bytes 3145728

commit v5 on v4

--- a/solution.py
+++ b/solution.py
@@ -8,7 +8,6 @@
 from jax.sharding import PartitionSpec as P
 
 HALF = 2
-UNROLL = True
 TN = 256
 NX = 4
 MESH = pl.DeviceIdType.MESH
@@ -17,7 +16,7 @@
 def kernel(
     ny, nz, ints_in, coef_in, vir_in, occ_in, kap_in, out_ref,
     ints, coef_ref, vir_ref, occ_ref, kap_ref, full, mine, gath, tit, row_exp, vir2, kvec, row_e, amp, acc,
-    in_sem, a_send, a_recv, g_send, g_recv, s_send, s_recv,
+    in_sem, a_send, a_recv, e_send, g_send, g_recv, s_send, s_recv,
 ):
     wide = lax.axis_index("wide")
     batch = lax.axis_index("batch")
@@ -41,6 +40,12 @@
 
     sibling = at_wide(y, zh, 1 - core)
     left, right, over = dev_batch(-1, 0), dev_batch(1, 0), dev_batch(0, 1)
+    beyond = {
+        "wide": 2 * lax.rem(own_pair + 2 * zl - 1 + pairs, pairs) + core,
+        "batch": at_batch(0, 1),
+    }
+    centre, shared, other = 1, 2 * zl, 2 - 2 * zl
+    order = (centre, shared, other)
 
     barrier = pltpu.get_barrier_semaphore()
     far = sorted(
@@ -49,7 +54,7 @@
     )
     owners = [(lax.rem(y + dy, ny), lax.rem(zh + dz, nz)) for dy, dz in far]
     peers = [at_wide(yy, zz, core) for yy, zz in owners]
-    peers += [left, right, over, sibling]
+    peers += [left, right, over, sibling, beyond]
     for peer in peers:
         pl.semaphore_signal(barrier, inc=1, device_id=peer, device_id_type=MESH)
 
@@ -104,7 +109,7 @@
             device_id_type=MESH,
         )
 
-    for p in (1, 0, 2):
+    for p in order:
         pltpu.make_async_copy(
             mine.at[own_pair + p], gath.at[batch, p, y, zh, core], a_recv.at[p]
         ).start()
@@ -141,6 +146,20 @@
         return pltpu.make_async_remote_copy(
             src_ref=ref, dst_ref=ref, send_sem=g_send.at[p, slot], recv_sem=g_recv.at[p, slot],
             device_id=to, device_id_type=MESH,
+        )
+
+    def e_copy(k):
+        dx, p, to_p, slot = (
+            (-1, centre, other, 5),
+            (1, centre, other, 6),
+            (2, centre, other, 7),
+            (2, shared, centre, 7),
+        )[k]
+        b = at_batch(dx, 0)
+        return pltpu.make_async_remote_copy(
+            src_ref=gath.at[b, p, :, :, core], dst_ref=gath.at[b, to_p, :, :, core],
+            send_sem=e_send.at[k], recv_sem=g_recv.at[to_p, slot],
+            device_id=beyond, device_id_type=MESH,
         )
 
     sends = {
@@ -217,8 +236,8 @@
             damp = 1.0 - jnp.concatenate([grown] * 2, axis=1) * col_exp[q : q + 1, :]
             amp[pl.ds(q * 64, 64), :] = (scaled * (damp * damp)).astype(jnp.bfloat16)
 
-        def tile(n, carry):
-            at = n * tn if isinstance(n, int) else pl.multiple_of(n * tn, tn)
+        def tile(n):
+            at = n * tn
             rhs = jnp.concatenate([r0[pl.ds(at, tn), :], r1[pl.ds(at, tn), :]], axis=1)
             part = lax.dot_general(
                 amp[...], rhs, (((1,), (1,)), ((), ())), preferred_element_type=jnp.float32
@@ -229,13 +248,9 @@
                 out_ref[:, pl.ds(at, tn)] = (acc[:, pl.ds(at, tn)] + part).astype(jnp.bfloat16)
             else:
                 acc[:, pl.ds(at, tn)] += part
-            return carry
-
-        if UNROLL:
-            for n in range(naux // tn):
-                tile(n, 0)
-        else:
-            lax.fori_loop(0, naux // tn, tile, 0)
+
+        for n in range(naux // tn):
+            tile(n)
 
     def own(p):
         a_wait(p)
@@ -250,17 +265,25 @@
         g_wait(p, 1)
         g_start(p, 4)
         s_start(p, 2)
+        if p is centre:
+            e_copy(0).start()
+            e_copy(1).start()
 
     def across(p):
         g_wait(p, 2)
-        g_start(p, 5)
-        g_start(p, 6)
+        if p is not shared:
+            g_start(p, 5)
+            g_start(p, 6)
         s_start(p, 3)
 
     def opposite(p):
         g_wait(p, 3)
         g_wait(p, 4)
-        g_start(p, 7)
+        if p is centre:
+            e_copy(2).start()
+        elif p is shared:
+            e_copy(3).start()
+            g_start(p, 7)
         s_start(p, 4)
 
     def corners(p):
@@ -274,56 +297,54 @@
 
     def step(p, first_block, second_block, first=False, last=False):
         for block in (first_block, second_block):
-            s_wait(p, block)
+            if (p is centre, block) != (True, 0):
+                s_wait(p, block)
         compute(p, first_block, second_block, first, last)
 
-    def compute_own(p):
-        if p != 1:
-            s_wait(p, 0)
-        s_wait(p, 3)
-        compute(p, 0, 3, False, False)
-
-    own(1)
-    own(0)
-    near(1)
-    own(2)
-    s_wait(1, 0)
-    tit[...] = jnp.transpose(flat(batch, 1)[...])
-    step(1, 1, 2, first=True)
-    near(0)
-    step(0, 1, 2)
-    near(2)
-    across(1)
-    compute_own(1)
-    opposite(1)
-    step(2, 1, 2)
-    across(0)
-    compute_own(0)
-    corners(1)
-    opposite(0)
-    across(2)
-    step(1, 5, 6)
-    compute_own(2)
-    far_corner(1)
-    step(1, 4, 7)
-    corners(0)
-    opposite(2)
-    step(0, 5, 6)
-    far_corner(0)
-    step(0, 4, 7)
-    corners(2)
-    step(2, 5, 6)
-    far_corner(2)
-    step(2, 4, 7, last=True)
+    own(centre)
+    own(shared)
+    near(centre)
+    own(other)
+    s_wait(centre, 0)
+    tit[...] = jnp.transpose(flat(batch, centre)[...])
+    step(centre, 1, 2, first=True)
+    near(shared)
+    step(shared, 1, 2)
+    near(other)
+    across(centre)
+    opposite(centre)
+    step(centre, 0, 3)
+    step(other, 1, 2)
+    opposite(shared)
+    across(other)
+    step(other, 0, 3)
+    corners(shared)
+    step(shared, 5, 6)
+    opposite(other)
+    across(shared)
+    corners(centre)
+    step(shared, 0, 3)
+    step(centre, 5, 6)
+    far_corner(shared)
+    step(shared, 4, 7)
+    far_corner(centre)
+    far_corner(other)
+    step(centre, 4, 7)
+    corners(other)
+    step(other, 4, 7)
+    step(other, 5, 6, last=True)
 
     for p in range(3):
         sent = mine.at[pl.ds(0, pairs - 1)]
         pltpu.make_async_copy(sent, sent, a_send.at[p]).wait()
-        for slot in range(8):
+        for block in range(8):
+            s_copy(p, block, core).wait_send()
+    for p, slots in ((centre, range(7)), (shared, (0, 1, 2, 3, 4, 7)), (other, range(7))):
+        for slot in slots:
             to, dx, dz, part = sends[slot]
             g_copy(p, dx, dz, part, slot, to).wait_send()
-        for block in range(8):
-            s_copy(p, block, core).wait_send()
+    for k in range(4):
+        e_copy(k).wait_send()
 
 
 def on_device(ny, nz, integrals, vir_coeff, occ_energy, vir_energy, kappas):
@@ -358,6 +379,7 @@
             dma((8,)),
             dma((3,)),
             dma((3,)),
+            dma((4,)),
             dma((3, 8)),
             dma((3, 8)),
             dma((3, 8)),

time: 69.8 us -> 65.4 us (0.937); the launches traced: 69.7 us -> 64.2 us
  Pallas kernels: 68.5 us -> 63.1 us
    pallas_call x1, Pallas kernels: 68.5 us -> 63.1 us  [on_device(): pl.pallas_call(functools.partial(kernel, ny, nz), out_shape=pltpu.VMEM((8...]
where the time goes in v5:
time: 65.4 us; the launch traced here: 64.2 us
  Pallas kernels  63.1 us (96%)
  local copies, waits for them, and re-layouts  1.15 us (2%)
    pallas_call x1, Pallas kernels, on_device(): pl.pallas_call(functools.partial(kernel, ny, nz), out_shape=pltpu.VMEM((8...  63.1 us

profile of v5, /device:TPU:1, one launch (start us, length us, event | category | flops | bytes accessed | tf_op | source)
XLA Modules:
  0.0 64.2 jit_solution(642068893308306150)
XLA Ops:
  0.0 63.1 %shard_map.55 = bf16[512,1536]{1,0:T(8,128)(2,1)S(1)} custom-call(bf16[1536,640]{1,0:T(8,128)(2,1)} %bitcast.7, bf16[64,640]{1,0:T(8,128)(2,1)} %bitcast.8, f32[1,512]{1,0:T(1,128)} %bitcast.9, f32[64]{0:T(128)} %occ_in.1, f32[8]{0:T(128)} %kap_in.1), custom_call_target="tpu_custom_call" | custom-call | tf_op jit(solution)/shard_map/pallas_call | solution.py:358
  63.1 1.1 %copy.8 = bf16[8,1,64,1536]{3,2,1,0:T(8,128)(2,1)} copy(bf16[8,1,64,1536]{3,2,1,0:T(8,128)(2,1)S(1)} %bitcast.6) | data formatting | bytes 3145728

commit v6 on v5

--- a/solution.py
+++ b/solution.py
@@ -16,7 +16,7 @@
 def kernel(
     ny, nz, ints_in, coef_in, vir_in, occ_in, kap_in, out_ref,
     ints, coef_ref, vir_ref, occ_ref, kap_ref, full, mine, gath, tit, row_exp, vir2, kvec, row_e, amp, acc,
-    in_sem, a_send, a_recv, e_send, g_send, g_recv, s_send, s_recv,
+    in_sem, a_send, a_recv, c_recv, e_send, g_send, g_recv, s_send, s_recv,
 ):
     wide = lax.axis_index("wide")
     batch = lax.axis_index("batch")
@@ -104,14 +104,15 @@
             src_ref=mine.at[yy * nz + zz + p],
             dst_ref=gath.at[batch, p, y, zh, core],
             send_sem=a_send.at[p],
-            recv_sem=a_recv.at[p],
+            recv_sem=c_recv.at[y] if p is centre else a_recv.at[p],
             device_id=at_wide(yy, zz, core),
             device_id_type=MESH,
         )
 
     for p in order:
         pltpu.make_async_copy(
-            mine.at[own_pair + p], gath.at[batch, p, y, zh, core], a_recv.at[p]
+            mine.at[own_pair + p], gath.at[batch, p, y, zh, core],
+            c_recv.at[y] if p is centre else a_recv.at[p],
         ).start()
         for yy, zz in owners:
             a_copy(p, yy, zz).start()
@@ -253,17 +254,32 @@
             tile(n)
 
     def own(p):
-        a_wait(p)
-        for slot in (0, 1, 2):
-            g_start(p, slot)
+        if p is centre:
+            for d in sorted(range(ny), key=lambda d: min(d, ny - d)):
+                row = lax.rem(y + d, ny)
+                ref = gath.at[batch, p, row, :, core]
+                pltpu.make_async_copy(ref, ref, c_recv.at[row]).wait()
+                for slot in (0, 1):
+                    pltpu.make_async_remote_copy(
+                        src_ref=ref, dst_ref=ref,
+                        send_sem=g_send.at[p, slot], recv_sem=g_recv.at[p, slot],
+                        device_id=sends[slot][0], device_id_type=MESH,
+                    ).start()
+        else:
+            a_wait(p)
+            g_start(p, 0)
+            g_start(p, 1)
+        g_start(p, 2)
         s_start(p, 0)
 
     def near(p):
         g_wait(p, 0)
-        g_start(p, 3)
+        if p is not other:
+            g_start(p, 3)
         s_start(p, 1)
         g_wait(p, 1)
-        g_start(p, 4)
+        if p is not other:
+            g_start(p, 4)
         s_start(p, 2)
         if p is centre:
             e_copy(0).start()
@@ -274,6 +290,9 @@
         if p is not shared:
             g_start(p, 5)
             g_start(p, 6)
+        if p is other:
+            g_start(p, 3)
+            g_start(p, 4)
         s_start(p, 3)
 
     def opposite(p):
@@ -307,32 +326,32 @@
     own(other)
     s_wait(centre, 0)
     tit[...] = jnp.transpose(flat(batch, centre)[...])
+    near(shared)
     step(centre, 1, 2, first=True)
-    near(shared)
-    step(shared, 1, 2)
     near(other)
     across(centre)
+    step(shared, 1, 2)
     opposite(centre)
     step(centre, 0, 3)
+    across(other)
+    opposite(shared)
+    corners(shared)
     step(other, 1, 2)
-    opposite(shared)
-    across(other)
     step(other, 0, 3)
-    corners(shared)
     step(shared, 5, 6)
-    opposite(other)
     across(shared)
+    far_corner(shared)
     corners(centre)
     step(shared, 0, 3)
+    step(shared, 4, 7)
+    corners(other)
     step(centre, 5, 6)
-    far_corner(shared)
-    step(shared, 4, 7)
     far_corner(centre)
     far_corner(other)
+    opposite(other)
+    step(other, 5, 6)
     step(centre, 4, 7)
-    corners(other)
-    step(other, 4, 7)
-    step(other, 5, 6, last=True)
+    step(other, 4, 7, last=True)
 
     for p in range(3):
         sent = mine.at[pl.ds(0, pairs - 1)]
@@ -379,6 +398,7 @@
             dma((8,)),
             dma((3,)),
             dma((3,)),
+            dma((ny,)),
             dma((4,)),
             dma((3, 8)),
             dma((3, 8)),

time: 65.4 us -> 61.4 us (0.939); the launches traced: 64.2 us -> 61.3 us
  Pallas kernels: 63.1 us -> 60.2 us
    pallas_call x1, Pallas kernels: 63.1 us -> 60.2 us  [on_device(): pl.pallas_call(functools.partial(kernel, ny, nz), out_shape=pltpu.VMEM((8...]
where the time goes in v6:
time: 61.4 us; the launch traced here: 61.3 us
  Pallas kernels  60.2 us (98%)
  local copies, waits for them, and re-layouts  1.15 us (2%)
    pallas_call x1, Pallas kernels, on_device(): pl.pallas_call(functools.partial(kernel, ny, nz), out_shape=pltpu.VMEM((8...  60.2 us

profile of v6, /device:TPU:1, one launch (start us, length us, event | category | flops | bytes accessed | tf_op | source)
XLA Modules:
  0.0 61.3 jit_solution(11850744320140064434)
XLA Ops:
  0.0 60.2 %shard_map.55 = bf16[512,1536]{1,0:T(8,128)(2,1)S(1)} custom-call(bf16[1536,640]{1,0:T(8,128)(2,1)} %bitcast.7, bf16[64,640]{1,0:T(8,128)(2,1)} %bitcast.8, f32[1,512]{1,0:T(1,128)} %bitcast.9, f32[64]{0:T(128)} %occ_in.1, f32[8]{0:T(128)} %kap_in.1), custom_call_target="tpu_custom_call" | custom-call | tf_op jit(solution)/shard_map/pallas_call | solution.py:377
  60.2 1.1 %copy.8 = bf16[8,1,64,1536]{3,2,1,0:T(8,128)(2,1)} copy(bf16[8,1,64,1536]{3,2,1,0:T(8,128)(2,1)S(1)} %bitcast.6) | data formatting | bytes 3145728
